TPU v7x, 32 devices: a whole 2x2x4 slice. The times are simulated.
32 devices in a mesh: parts: 2 (over x), blocks: 16 (over z, y, core).
Axes of the slice: x: 2, y: 2, z: 4, core: 2. Of those that a mesh axis runs over, the one named last changes fastest.
Arguments:
- coords: float32 [640, 3, 32768], P('blocks', None, 'parts'), parts along dimension 2
- pairs: int32 [2, 2048], replicated, may hold values from 0 to 639
- res_slot: int32 [640], replicated, may hold values from 0 to 639, each once
Outputs:
- distances: bfloat16 [4, 32768, 1024], P(None, ('parts', 'blocks')), parts along dimension 1
There are 2 independent parts, one for each index of `parts`. A program takes and returns all parts, laid end to end along the dimension named above; an argument that names none is the same for every part. Nothing has to cross between parts.
All inputs are finite; a program needn't handle non-finite values.
Results may differ from a plain program's by a relative error of at most 0.0025.
Values may be sent and summed in bfloat16 or wider, within the bound.
No kernel may reach another device: no remote copies, remote signals or barrier semaphores. Data moves between devices by JAX's collectives and lax.ppermute only.
A program may use at most 192 MiB of HBM per device.

v0:
```python
import jax
import jax.numpy as jnp
from jax import lax
from jax.sharding import PartitionSpec as P

ROUNDS = 4


def shifted(shard, axis, by):
    count = lax.axis_size(axis)
    return lax.ppermute(shard, axis, [(i, (i + by) % count) for i in range(count)])


def row_norms(features):
    wide = features.astype(jnp.float32)
    return jnp.sum(wide * wide, axis=1)


def shards(coords, pairs, res_slot):
    width_blocks = lax.axis_size("blocks")
    res_local, _, frames = coords.shape
    per_block = frames // width_blocks
    residues = res_local * width_blocks
    position = (
        jnp.zeros((residues,), jnp.int32).at[res_slot].set(jnp.arange(residues, dtype=jnp.int32))
    )
    slot_first = position[pairs[0]]
    slot_second = position[pairs[1]]
    split_coords = coords.reshape(res_local, 3, width_blocks, per_block)
    gathered = lax.all_to_all(split_coords, "blocks", split_axis=2, concat_axis=0, tiled=True)
    squared = jnp.zeros((slot_first.shape[0], gathered.shape[3]), jnp.float32)
    for component in range(3):
        offset = gathered[slot_first, component, 0] - gathered[slot_second, component, 0]
        squared = squared + offset * offset
    separation = jnp.sqrt(squared + 0.01)
    features = jax.nn.sigmoid((8.0 - separation) / 1.5).T.astype(jnp.bfloat16)
    own_norms = row_norms(features)
    results = []
    visitor = features
    for offset_round in range(1, ROUNDS + 1):
        visitor = shifted(visitor, "blocks", 1)
        vis_norms = row_norms(visitor)
        intersection = lax.dot_general(
            features, visitor, (((1,), (1,)), ((), ())), preferred_element_type=jnp.float32
        )
        ratio = intersection / (own_norms[:, None] + vis_norms[None, :] - intersection + 1e-06)
        results.append((1.0 - ratio).astype(jnp.bfloat16))
    return jnp.stack(results)


def solution(mesh):
    in_specs = (P("blocks", None, "parts"), P(), P())
    out_specs = P(None, ("parts", "blocks"), None)
    return jax.shard_map(shards, mesh=mesh, in_specs=in_specs, out_specs=out_specs, check_vma=False)
```

profile of v0, /device:TPU:0, one launch (start us, length us, event | category | flops | bytes accessed | tf_op | source)
XLA Modules:
  0.0 669.1 jit_solution(15430760271793867332)
XLA Ops:
  0.0 8.0 %copy.15 = f32[3,5,16,8,1024]{4,3,1,0,2:T(8,128)} copy(f32[3,5,16,8,1024]{4,3,2,1,0:T(8,128)} %bitcast.54) | data formatting | bytes 15728640 | tf_op jit(solution)/shard_map/reshape | solution.py:29
  8.0 0.0 copy-start.2
  8.0 0.0 copy-start.1
  8.0 7.6 %all-to-all-start = ((f32[40,3,16,1024]{3,0,1,2:T(8,128)}), f32[40,3,16,1024]{3,0,1,2:T(8,128)}, u32[]{:S(2)}, u32[]{:S(2)}) async-start(f32[40,3,16,1024]{3,0,1,2:T(8,128)} %bitcast.53), calls=%async_computation | async-start | bytes 15728640 | tf_op jit(solution)/shard_map/all_to_all | solution.py:30
  15.6 0.0 copy-done.2
  15.6 4.3 scatter_custom_fusion
  19.9 0.0 copy-done.1
  20.0 8.6 %gather_fusion.2 = s32[2048]{0:T(1024)S(1)} fusion(s32[640]{0:T(1024)S(1)} %scatter_custom_fusion, s32[2048]{0:T(1024)S(1)} %broadcast_clamp_fusion), kind=kCustom, calls=%fused_computation.2 | custom fusion | bytes 24576 | tf_op jit(solution)/shard_map/gather | solution.py:28
  28.6 8.6 %gather_fusion = s32[2048]{0:T(1024)S(1)} fusion(s32[640]{0:T(1024)S(1)} %scatter_custom_fusion, s32[2048]{0:T(1024)S(1)} %broadcast_clamp_fusion.1), kind=kCustom, calls=%fused_computation | custom fusion | bytes 24576 | tf_op jit(solution)/shard_map/gather | solution.py:27
  37.2 119.8 %all-to-all-done = f32[40,3,16,1024]{3,0,1,2:T(8,128)} async-done(((f32[40,3,16,1024]{3,0,1,2:T(8,128)}), f32[40,3,16,1024]{3,0,1,2:T(8,128)}, u32[]{:S(2)}, u32[]{:S(2)}) %all-to-all-start) | async-done | bytes 7864352 | tf_op jit(solution)/shard_map/all_to_all | solution.py:30
  157.0 10.7 %copy.11 = f32[16,40,3,1,1024]{4,3,2,1,0:T(1,128)} copy(f32[16,40,3,1,1024]{4,1,2,0,3:T(8,128)} %bitcast.2) | data formatting | bytes 15728640 | tf_op jit(solution)/shard_map/all_to_all | solution.py:30
  167.7 38.9 %gather_fusion.7 = f32[2048,1024]{1,0:T(8,128)} fusion(f32[640,3,1,1024]{3,2,1,0:T(1,128)} %bitcast.41, s32[2048]{0:T(1024)S(1)} %bitcast.52), kind=kCustom, calls=%fused_computation.7 | custom fusion | bytes 16801792 | tf_op jit(solution)/shard_map/gather | solution.py:33
  206.7 38.8 %gather_fusion.6 = f32[2048,1024]{1,0:T(8,128)} fusion(f32[640,3,1,1024]{3,2,1,0:T(1,128)} %bitcast.42, s32[2048]{0:T(1024)S(1)} %bitcast.51), kind=kCustom, calls=%fused_computation.6 | custom fusion | bytes 16801792 | tf_op jit(solution)/shard_map/gather | solution.py:33
  245.4 38.9 %gather_fusion.5 = f32[2048,1024]{1,0:T(8,128)} fusion(f32[640,3,1,1024]{3,2,1,0:T(1,128)} %bitcast.43, s32[2048]{0:T(1024)S(1)} %bitcast.50), kind=kCustom, calls=%fused_computation.5 | custom fusion | bytes 16801792 | tf_op jit(solution)/shard_map/gather | solution.py:33
  284.4 39.1 %gather_fusion.4 = f32[2048,1024]{1,0:T(8,128)} fusion(f32[640,3,1,1024]{3,2,1,0:T(1,128)} %bitcast.44, s32[2048]{0:T(1024)S(1)} %bitcast.49), kind=kCustom, calls=%fused_computation.4 | custom fusion | bytes 16801792 | tf_op jit(solution)/shard_map/gather | solution.py:33
  323.5 38.9 %gather_fusion.3 = f32[2048,1024]{1,0:T(8,128)} fusion(f32[640,3,1,1024]{3,2,1,0:T(1,128)} %bitcast.45, s32[2048]{0:T(1024)S(1)} %bitcast.48), kind=kCustom, calls=%fused_computation.3 | custom fusion | bytes 16801792 | tf_op jit(solution)/shard_map/gather | solution.py:33
  362.4 39.2 %gather_fusion.1 = f32[2048,1024]{1,0:T(8,128)} fusion(f32[640,3,1,1024]{3,2,1,0:T(1,128)} %bitcast.46, s32[2048]{0:T(1024)S(1)} %bitcast.47), kind=kCustom, calls=%fused_computation.1 | custom fusion | bytes 16801792 | tf_op jit(solution)/shard_map/gather | solution.py:33
  401.5 21.2 %multiply_reduce_fusion.4 = (f32[1024]{0:T(1024)S(1)}, bf16[2048,1024]{1,0:T(8,128)(2,1)}) fusion(f32[2048,1024]{1,0:T(8,128)} %gather_fusion.6, f32[2048,1024]{1,0:T(8,128)} %gather_fusion.7, f32[2048,1024]{1,0:T(8,128)} %gather_fusion.4, f32[2048,1024]{1,0:T(8,128)} %gather_fusion.5, f32[2048,1024]{1,0:T(8,128)} %gather_fusion.1, f32[2048,1024]{1,0:T(8,128)} %gather_fusion.3), kind=kLoop, calls=%fused_computation.15 | loop fusion | flops 37747712 | bytes 54530048 | tf_op jit(solution)/shard_map/reduce_sum | solution.py:16
  422.7 0.0 copy-start
  422.7 1.0 collective-permute-start
  423.7 78.5 %collective-permute-done = bf16[1024,2048]{0,1:T(8,128)(2,1)S(1)} collective-permute-done((bf16[1024,2048]{0,1:T(8,128)(2,1)}, bf16[1024,2048]{0,1:T(8,128)(2,1)S(1)}, u32[]{:S(2)}, u32[]{:S(2)}) %collective-permute-start) | collective-permute-done | bytes 4194336 | tf_op jit(solution)/shard_map/ppermute | solution.py:11
  502.2 0.0 collective-permute-start.1
  502.2 50.6 %collective-permute-done.1 = bf16[1024,2048]{0,1:T(8,128)(2,1)S(1)} collective-permute-done((bf16[1024,2048]{0,1:T(8,128)(2,1)S(1)}, bf16[1024,2048]{0,1:T(8,128)(2,1)S(1)}, u32[]{:S(2)}, u32[]{:S(2)}) %collective-permute-start.1) | collective-permute-done | bytes 4194336 | tf_op jit(solution)/shard_map/ppermute | solution.py:11
  552.8 0.0 collective-permute-start.2
  552.8 50.6 %collective-permute-done.2 = bf16[1024,2048]{0,1:T(8,128)(2,1)S(1)} collective-permute-done((bf16[1024,2048]{0,1:T(8,128)(2,1)S(1)}, bf16[1024,2048]{0,1:T(8,128)(2,1)S(1)}, u32[]{:S(2)}, u32[]{:S(2)}) %collective-permute-start.2) | collective-permute-done | bytes 4194336 | tf_op jit(solution)/shard_map/ppermute | solution.py:11
  603.5 0.0 collective-permute-start.3
  603.5 0.9 multiply_reduce_fusion.3
  604.4 0.0 copy-done
  604.4 4.7 fusion.12
  609.2 0.9 multiply_reduce_fusion.2
  610.1 6.4 fusion.13
  616.5 0.9 multiply_reduce_fusion.1
  617.4 6.2 fusion.14
  623.6 30.5 %collective-permute-done.3 = bf16[1024,2048]{0,1:T(8,128)(2,1)S(1)} collective-permute-done((bf16[1024,2048]{0,1:T(8,128)(2,1)S(1)}, bf16[1024,2048]{0,1:T(8,128)(2,1)S(1)}, u32[]{:S(2)}, u32[]{:S(2)}) %collective-permute-start.3) | collective-permute-done | bytes 4194336 | tf_op jit(solution)/shard_map/ppermute | solution.py:11
  654.1 0.9 multiply_reduce_fusion
  655.0 10.2 %fusion = (bf16[1,1024,1024]{2,1,0:T(8,128)(2,1)S(1)}, bf16[1,1024,1024]{2,1,0:T(8,128)(2,1)S(1)}, bf16[1,1024,1024]{2,1,0:T(8,128)(2,1)S(1)}, bf16[1,1024,1024]{2,1,0:T(8,128)(2,1)S(1)}) fusion(f32[1024,1024]{1,0:T(8,128)S(1)} %fusion.12, f32[1024]{0:T(1024)S(1)} %multiply_reduce_fusion.3, f32[1024]{0:T(1024)S(1)} %get-tuple-element.5, ...), kind=kOutput, calls=%fused_computation.21 | convolution fusion | flops 4320133120 | bytes 29380608 | tf_op jit(solution)/shard_map/dot_general | solution.py:43
  665.2 3.9 pad_maximum_fusion
  (9 shorter events, 0.1 us)
Async XLA Ops:
  8.0 7.6 %copy-start.2 = (s32[640]{0:T(1024)S(1)}, s32[640]{0:T(1024)}, u32[]{:S(2)}) copy-start(s32[640]{0:T(1024)} %param.5) | copy-start | bytes 7684
  8.0 11.9 %copy-start.1 = (s32[2,2048]{1,0:T(2,128)S(1)}, s32[2,2048]{1,0:T(2,128)}, u32[]{:S(2)}) copy-start(s32[2,2048]{1,0:T(2,128)} %param.4) | copy-start | bytes 49156
  8.0 149.0 %all-to-all-start = ((f32[40,3,16,1024]{3,0,1,2:T(8,128)}), f32[40,3,16,1024]{3,0,1,2:T(8,128)}, u32[]{:S(2)}, u32[]{:S(2)}) async-start(f32[40,3,16,1024]{3,0,1,2:T(8,128)} %bitcast.53), calls=%async_computation | async-start | bytes 15728640 | tf_op jit(solution)/shard_map/all_to_all | solution.py:30
  422.7 181.7 %copy-start = (bf16[2048,1024]{1,0:T(8,128)(2,1)S(1)}, bf16[2048,1024]{1,0:T(8,128)(2,1)}, u32[]{:S(2)}) copy-start(bf16[2048,1024]{1,0:T(8,128)(2,1)} %get-tuple-element.6) | copy-start | bytes 12582916
  422.7 79.5 %collective-permute-start = (bf16[1024,2048]{0,1:T(8,128)(2,1)}, bf16[1024,2048]{0,1:T(8,128)(2,1)S(1)}, u32[]{:S(2)}, u32[]{:S(2)}) collective-permute-start(bf16[1024,2048]{0,1:T(8,128)(2,1)} %bitcast.55), channel_id=1, source_target_pairs={{0,1},{1,2},{2,3},{3,4},{4,5},{5,6},{6,7},{7,8},{8,9},{9,10},{10,1... | collective-permute-start | bytes 12582920 | tf_op jit(solution)/shard_map/ppermute | solution.py:11
  502.2 50.6 %collective-permute-start.1 = (bf16[1024,2048]{0,1:T(8,128)(2,1)S(1)}, bf16[1024,2048]{0,1:T(8,128)(2,1)S(1)}, u32[]{:S(2)}, u32[]{:S(2)}) collective-permute-start(bf16[1024,2048]{0,1:T(8,128)(2,1)S(1)} %collective-permute-done), channel_id=1, source_target_pairs={{0,1},{1,2},{2,3},{3,4},{4,5},{5,6},{6,7},{7,8},{8,9},{9,10},{10,1... | collective-permute-start | bytes 12582920 | tf_op jit(solution)/shard_map/ppermute | solution.py:11
  552.8 50.6 %collective-permute-start.2 = (bf16[1024,2048]{0,1:T(8,128)(2,1)S(1)}, bf16[1024,2048]{0,1:T(8,128)(2,1)S(1)}, u32[]{:S(2)}, u32[]{:S(2)}) collective-permute-start(bf16[1024,2048]{0,1:T(8,128)(2,1)S(1)} %collective-permute-done.1), channel_id=1, source_target_pairs={{0,1},{1,2},{2,3},{3,4},{4,5},{5,6},{6,7},{7,8},{8,9},{9,10},{10,1... | collective-permute-start | bytes 12582920 | tf_op jit(solution)/shard_map/ppermute | solution.py:11
  603.5 50.6 %collective-permute-start.3 = (bf16[1024,2048]{0,1:T(8,128)(2,1)S(1)}, bf16[1024,2048]{0,1:T(8,128)(2,1)S(1)}, u32[]{:S(2)}, u32[]{:S(2)}) collective-permute-start(bf16[1024,2048]{0,1:T(8,128)(2,1)S(1)} %collective-permute-done.2), channel_id=1, source_target_pairs={{0,1},{1,2},{2,3},{3,4},{4,5},{5,6},{6,7},{7,8},{8,9},{9,10},{10,1... | collective-permute-start | bytes 12582920 | tf_op jit(solution)/shard_map/ppermute | solution.py:11
where the time goes:
time: 673 us; the launch traced here: 669 us
  waiting for transfers between devices  330 us (49%)
  local copies, waits for them, and re-layouts  274 us (41%)
  other arithmetic  28.9 us (4%)
  matrix products  27.5 us (4%)
  starting transfers between devices  8.57 us (1%)
    ppermute x4, waiting for transfers between devices, shifted(): lax.ppermute(shard, axis, [(i, (i + by) % count) for i in range(count)])  210 us
    all_to_all x1, waiting for transfers between devices, shards(): lax.all_to_all(split_coords, 'blocks', split_axis=2, concat_axis=0, tiled...  120 us
    gather x3, local copies, waits for them, and re-layouts, shards(): gathered[slot_first, component, 0] - gathered[slot_second, component, 0]  117 us
    gather x3, local copies, waits for them, and re-layouts, shards(): gathered[slot_second, component, 0]  117 us
    dot_general x4, matrix products, shards(): lax.dot_general(features, visitor, (((1,), (1,)), ((), ())), preferred_el...  27.5 us
    reduce_sum x5, other arithmetic, row_norms(): return jnp.sum(wide * wide, axis=1)  24.9 us
  transfers between devices with their start and end apart: 5, of which 5 were waited for; matrix products, arithmetic and copies ran while one was open for 6% of the time, Pallas kernels for 0%

commit v1 on v0

v1 whole, which is shorter than its diff:
```python
import functools

import jax
import jax.numpy as jnp
from jax import lax
from jax.experimental import pallas as pl
from jax.experimental.pallas import tpu as pltpu
from jax.sharding import PartitionSpec as P

ROUNDS = 4
CHUNKS = 4
BF16_MAX = 3.3895313892515355e38


def permuted(shard, axis, to):
    count = lax.axis_size(axis)
    return lax.ppermute(shard, axis, [(i, to(i, count)) for i in range(count)])


def shift4(i, count):
    return (i + 4) % count


def swap1(i, count):
    return i ^ 1


def swap2(i, count):
    return i ^ 2


def features_kernel(x_ref, sel_ref, *refs, aliased):
    refs = refs[1:] if aliased else refs
    ft_ref, f_ref, norm_ref, split_ref = refs
    step = pl.program_id(0)
    groups, _, rows, width = x_ref.shape
    residues = groups * rows

    @pl.when(step == 0)
    def _():
        for component in range(3):
            rest = x_ref[:, component].reshape(residues, width)
            for term in range(3):
                part = jnp.clip(rest, -BF16_MAX, BF16_MAX).astype(jnp.bfloat16)
                split_ref[component, term * residues:(term + 1) * residues, :] = part
                rest = rest - part.astype(jnp.float32)
        norm_ref[...] = jnp.zeros_like(norm_ref)

    sel = sel_ref[...]
    sel = jnp.concatenate([sel, sel, sel], axis=1)
    squared = None
    for component in range(3):
        offset = jnp.dot(sel, split_ref[component], preferred_element_type=jnp.float32)
        squared = offset * offset if squared is None else squared + offset * offset
    separation = jnp.sqrt(squared + 0.01)
    feature = jax.nn.sigmoid((8.0 - separation) * (1.0 / 1.5)).astype(jnp.bfloat16)
    ft_ref[...] = feature
    own = feature.astype(jnp.float32).T
    f_ref[...] = own.astype(jnp.bfloat16)
    norm_ref[...] += jnp.sum(own * own, axis=1, keepdims=True)


def features_chunk(x, sel, own, chunk, chunks):
    groups, _, rows, width = x.shape
    contacts, residues = sel.shape
    tile = 256
    aliased = own is not None
    in_specs = [
        pl.BlockSpec(x.shape, lambda i: (0, 0, 0, 0)),
        pl.BlockSpec((tile, residues), lambda i: (i, 0)),
    ]
    args = [x, sel]
    if aliased:
        in_specs.append(pl.BlockSpec(memory_space=pl.ANY))
        args.append(own)
    return pl.pallas_call(
        functools.partial(features_kernel, aliased=aliased),
        grid=(contacts // tile,),
        in_specs=in_specs,
        out_specs=[
            pl.BlockSpec((tile, width), lambda i: (i, 0)),
            pl.BlockSpec((width, tile), lambda i: (chunk, i)),
            pl.BlockSpec((width, 1), lambda i: (0, 0)),
        ],
        out_shape=[
            jax.ShapeDtypeStruct((contacts, width), jnp.bfloat16),
            jax.ShapeDtypeStruct((width * chunks, contacts), jnp.bfloat16),
            jax.ShapeDtypeStruct((width, 1), jnp.float32),
        ],
        scratch_shapes=[pltpu.VMEM((3, 3 * residues, width), jnp.bfloat16)],
        input_output_aliases={2: 1} if aliased else {},
        name=f"features_{chunk}",
    )(*args)


def distance_kernel(bit_ref, own_ref, norm_ref, v4_ref, v2_ref, vx_ref, *refs, aliased):
    refs = refs[1:] if aliased else refs
    out_ref, vnorm_ref = refs
    bit = bit_ref[0]
    visitors = (
        lambda: vx_ref[bit],
        lambda: v2_ref[...],
        lambda: vx_ref[1 - bit],
        lambda: v4_ref[...],
    )

    @pl.when(pl.program_id(0) == 0)
    def _():
        for r, load in enumerate(visitors):
            wide = load().astype(jnp.float32)
            vnorm_ref[r, 0:1, :] = jnp.sum(wide * wide, axis=0, keepdims=True)

    own = own_ref[...]
    own_norm = norm_ref[...]
    for r, load in enumerate(visitors):
        inter = jnp.dot(own, load(), preferred_element_type=jnp.float32)
        ratio = inter / (own_norm + vnorm_ref[r, 0:1, :] - inter + 1e-06)
        out_ref[r] = (1.0 - ratio).astype(jnp.bfloat16)


def distance_chunk(bit, own, norms, v4, v2, vx, out, chunk, chunks):
    frames, contacts = own.shape
    width = v4.shape[1]
    tile = 256
    aliased = out is not None
    in_specs = [
        pl.BlockSpec(memory_space=pltpu.SMEM),
        pl.BlockSpec((tile, contacts), lambda i: (i, 0)),
        pl.BlockSpec((tile, 1), lambda i: (i, 0)),
        pl.BlockSpec((contacts, width), lambda i: (0, 0)),
        pl.BlockSpec((contacts, width), lambda i: (0, 0)),
        pl.BlockSpec((2, contacts, width), lambda i: (0, 0, 0)),
    ]
    args = [bit, own, norms, v4, v2, vx]
    if aliased:
        in_specs.append(pl.BlockSpec(memory_space=pl.ANY))
        args.append(out)
    return pl.pallas_call(
        functools.partial(distance_kernel, aliased=aliased),
        grid=(frames // tile,),
        in_specs=in_specs,
        out_specs=pl.BlockSpec((ROUNDS, tile, width), lambda i: (0, i, chunk)),
        out_shape=jax.ShapeDtypeStruct((ROUNDS, frames, width * chunks), jnp.bfloat16),
        scratch_shapes=[pltpu.VMEM((ROUNDS, 8, width), jnp.float32)],
        input_output_aliases={6: 0} if aliased else {},
        name=f"distances_{chunk}",
    )(*args)


def shards(coords, pairs, res_slot):
    count = lax.axis_size("blocks")
    index = lax.axis_index("blocks")
    res_local, _, frames = coords.shape
    per_block = frames // count
    width = per_block // CHUNKS
    residues = res_local * count

    split_coords = coords.reshape(res_local, 3, count, CHUNKS, width)
    arrived = []
    for j in range(CHUNKS):
        piece = split_coords[:, :, :, j].transpose(2, 1, 0, 3)
        got = lax.all_to_all(piece, "blocks", split_axis=0, concat_axis=0, tiled=True)
        if res_local % 8:
            got = got.transpose(1, 0, 2, 3).reshape(1, 3, residues, width)
        arrived.append(got)

    first = (pairs[0][:, None] == res_slot[None, :]).astype(jnp.float32)
    second = (pairs[1][:, None] == res_slot[None, :]).astype(jnp.float32)
    sel = (first - second).astype(jnp.bfloat16)

    low_core = (index & 1) == 0
    low_pair = (index & 2) == 0
    bit = (index & 1).astype(jnp.int32).reshape(1)

    own = None
    norms, visitors = [], []
    for j in range(CHUNKS):
        ft, own, norm = features_chunk(arrived[j], sel, own, j, CHUNKS)
        norms.append(norm)
        v4 = permuted(ft, "blocks", shift4)
        v2 = permuted(jnp.where(low_pair, ft, v4), "blocks", swap2)
        vx = permuted(jnp.stack([v2, jnp.where(low_core, ft, v4)]), "blocks", swap1)
        visitors.append((v4, v2, vx))
    norms = jnp.concatenate(norms, axis=0)
    out = None
    for j in range(CHUNKS):
        out = distance_chunk(bit, own, norms, *visitors[j], out, j, CHUNKS)
    return out


def solution(mesh):
    in_specs = (P("blocks", None, "parts"), P(), P())
    out_specs = P(None, ("parts", "blocks"), None)
    return jax.shard_map(shards, mesh=mesh, in_specs=in_specs, out_specs=out_specs, check_vma=False)
```

time: 673 us -> 449 us (0.67)
  local copies, waits for them, and re-layouts: 274 us -> 47.1 us
  waiting for transfers between devices: 330 us -> 241 us
  Pallas kernels: 0 us -> 88.9 us
  starting transfers between devices: 8.57 us -> 58.5 us
  matrix products: 27.5 us -> 0 us
  other arithmetic: 28.9 us -> 11.9 us
    gather x8 -> x0, local copies, waits for them, and re-layouts: 251 us -> none  [the longest x3 117 us: shards(): gathered[slot_first, component, 0] - gathered[slot_second, component, 0]]
    ppermute x4 -> x12, waiting for transfers between devices: 210 us -> 78 us  [permuted(): return lax.ppermute(shard, axis, [(i, to(i, count)) for i in range(count)])]
    pallas_call x0 -> x8, Pallas kernels: none -> 88.9 us  [the longest x4 52.7 us: features_chunk(): pl.pallas_call(functools.partial(features_kernel, aliased=aliased), grid=...]
    all_to_all x1 -> x4, waiting for transfers between devices: 120 us -> 163 us  [shards(): lax.all_to_all(piece, 'blocks', split_axis=0, concat_axis=0, tiled=True)]
    all_to_all x1 -> x4, starting transfers between devices: 7.59 us -> 39.5 us  [shards(): lax.all_to_all(piece, 'blocks', split_axis=0, concat_axis=0, tiled=True)]
    dot_general x4 -> x0, matrix products: 27.5 us -> none  [shards(): lax.dot_general(features, visitor, (((1,), (1,)), ((), ())), preferred_el...]
    reduce_sum x5 -> x0, other arithmetic: 24.9 us -> none  [row_norms(): return jnp.sum(wide * wide, axis=1)]
    unnamed x6 -> x38, local copies, waits for them, and re-layouts: 0.01 us -> 18.9 us
  transfers between devices with their start and end apart: 5 -> 16, of which waited for: 5 -> 9; matrix products, arithmetic and copies ran while one was open for 6% -> 6% of each run, Pallas kernels for 0% -> 18%
where the time goes in v1:
time: 449 us; the launch traced here: 448 us
  waiting for transfers between devices  241 us (54%)
  Pallas kernels  88.9 us (20%)
  starting transfers between devices  58.5 us (13%)
  local copies, waits for them, and re-layouts  47.1 us (10%)
  other arithmetic  11.9 us (3%)
    all_to_all x4, waiting for transfers between devices, shards(): lax.all_to_all(piece, 'blocks', split_axis=0, concat_axis=0, tiled=True)  163 us
    ppermute x12, waiting for transfers between devices, permuted(): return lax.ppermute(shard, axis, [(i, to(i, count)) for i in range(count)])  78 us
    pallas_call x4, Pallas kernels, features_chunk(): pl.pallas_call(functools.partial(features_kernel, aliased=aliased), grid=...  52.7 us
    all_to_all x4, starting transfers between devices, shards(): lax.all_to_all(piece, 'blocks', split_axis=0, concat_axis=0, tiled=True)  39.5 us
    pallas_call x4, Pallas kernels, distance_chunk(): pl.pallas_call(functools.partial(distance_kernel, aliased=aliased), grid=...  36.1 us
    ppermute x12, starting transfers between devices, permuted(): return lax.ppermute(shard, axis, [(i, to(i, count)) for i in range(count)])  19 us
    unnamed x38, local copies, waits for them, and re-layouts  18.9 us
    slice x1, local copies, waits for them, and re-layouts, shards(): piece = split_coords[:, :, :, j].transpose(2, 1, 0, 3)  15.7 us
  transfers between devices with their start and end apart: 16, of which 9 were waited for; matrix products, arithmetic and copies ran while one was open for 6% of the time, Pallas kernels for 18%

profile of v1, /device:TPU:0, one launch (start us, length us, event | category | flops | bytes accessed | tf_op | source)
XLA Modules:
  0.0 447.9 jit_solution(8492565330301661611)
XLA Ops:
  0.0 10.2 %reshape.10 = f32[40,3,16,4,256]{4,3,2,0,1:T(4,128)} reshape(f32[40,3,16384]{2,0,1:T(8,128)} %param.3) | data formatting | bytes 15728640 | tf_op jit(solution)/shard_map/reshape | solution.py:158
  10.2 15.7 %fusion = (f32[40,3,16,1,256]{4,3,2,0,1:T(1,128)S(1)}, f32[40,3,16,1,256]{4,3,2,0,1:T(1,128)}, f32[40,3,16,1,256]{4,3,2,0,1:T(1,128)}, f32[40,3,16,1,256]{4,3,2,0,1:T(1,128)}) fusion(f32[40,3,16,4,256]{4,3,2,0,1:T(4,128)} %reshape.10), kind=kLoop, calls=%fused_computation.18 | loop fusion | bytes 15728640 | tf_op jit(solution)/shard_map/slice | solution.py:161
  25.9 2.4 copy.34
  28.3 7.4 %all-to-all-start.3 = ((f32[16,3,40,256]{3,2,1,0:T(8,128)}), f32[16,3,40,256]{3,2,1,0:T(8,128)S(1)}, u32[]{:S(2)}, u32[]{:S(2)}) async-start(f32[16,3,40,256]{3,2,1,0:T(8,128)} %bitcast.40), calls=%async_computation.3 | async-start | bytes 3932160 | tf_op jit(solution)/shard_map/all_to_all | solution.py:162
  35.8 3.9 copy.35
  39.7 34.7 %all-to-all-done.3.x_ref = f32[16,3,40,256]{3,2,1,0:T(8,128)S(1)} async-done(((f32[16,3,40,256]{3,2,1,0:T(8,128)}), f32[16,3,40,256]{3,2,1,0:T(8,128)S(1)}, u32[]{:S(2)}, u32[]{:S(2)}) %all-to-all-start.3) | async-done | bytes 1966112 | tf_op jit(solution)/shard_map/all_to_all | solution.py:162
  74.5 10.7 %all-to-all-start.2 = ((f32[16,3,40,256]{3,2,1,0:T(8,128)}), f32[16,3,40,256]{3,2,1,0:T(8,128)}, u32[]{:S(2)}, u32[]{:S(2)}) async-start(f32[16,3,40,256]{3,2,1,0:T(8,128)} %bitcast.39), calls=%async_computation.2 | async-start | bytes 3932160 | tf_op jit(solution)/shard_map/all_to_all | solution.py:162
  85.2 4.0 copy.36
  89.2 34.8 %all-to-all-done.2.x_ref = f32[16,3,40,256]{3,2,1,0:T(8,128)} async-done(((f32[16,3,40,256]{3,2,1,0:T(8,128)}), f32[16,3,40,256]{3,2,1,0:T(8,128)}, u32[]{:S(2)}, u32[]{:S(2)}) %all-to-all-start.2) | async-done | bytes 1966112 | tf_op jit(solution)/shard_map/all_to_all | solution.py:162
  124.0 10.7 %all-to-all-start.1 = ((f32[16,3,40,256]{3,2,1,0:T(8,128)}), f32[16,3,40,256]{3,2,1,0:T(8,128)S(1)}, u32[]{:S(2)}, u32[]{:S(2)}) async-start(f32[16,3,40,256]{3,2,1,0:T(8,128)} %bitcast.38), calls=%async_computation.1 | async-start | bytes 3932160 | tf_op jit(solution)/shard_map/all_to_all | solution.py:162
  134.7 4.0 copy.37
  138.7 34.7 %all-to-all-done.1.x_ref = f32[16,3,40,256]{3,2,1,0:T(8,128)S(1)} async-done(((f32[16,3,40,256]{3,2,1,0:T(8,128)}), f32[16,3,40,256]{3,2,1,0:T(8,128)S(1)}, u32[]{:S(2)}, u32[]{:S(2)}) %all-to-all-start.1) | async-done | bytes 1966112 | tf_op jit(solution)/shard_map/all_to_all | solution.py:162
  173.3 1.4 copy-done.1
  174.7 10.7 %all-to-all-start = ((f32[16,3,40,256]{3,2,1,0:T(8,128)}), f32[16,3,40,256]{3,2,1,0:T(8,128)S(1)}, u32[]{:S(2)}, u32[]{:S(2)}) async-start(f32[16,3,40,256]{3,2,1,0:T(8,128)} %bitcast.37), calls=%async_computation | async-start | bytes 3932160 | tf_op jit(solution)/shard_map/all_to_all | solution.py:162
  185.4 2.2 subtract_convert_fusion.sel_ref
  187.6 13.2 %features_0.1 = (bf16[2048,256]{1,0:T(8,128)(2,1)}, bf16[1024,2048]{1,0:T(8,128)(2,1)}, f32[256,1]{1,0:T(8,128)}) custom-call(f32[16,3,40,256]{3,2,1,0:T(8,128)} %copy-done.2, bf16[2048,640]{1,0:T(8,128)(2,1)} %subtract_convert_fusion.sel_ref), custom_call_target="tpu_custom_call" | custom-call | tf_op jit(solution)/shard_map/features_0/pallas_call | solution.py:76
  200.8 2.2 collective-permute-start.9
  203.0 13.2 %features_1.1 = (bf16[2048,256]{1,0:T(8,128)(2,1)}, bf16[1024,2048]{1,0:T(8,128)(2,1)}, f32[256,1]{1,0:T(8,128)}) custom-call(f32[16,3,40,256]{3,2,1,0:T(8,128)} %all-to-all-done.2.x_ref, bf16[2048,640]{1,0:T(8,128)(2,1)} %subtract_convert_fusion.sel_ref, bf16[1024,2048]{1,0:T(8,128)(2,1)} %get-tuple-element.17.refs_0_), custom_call_target="tpu_custom_call", output_to_operand_aliasing={{1}: (2, {})} | custom-call | tf_op jit(solution)/shard_map/features_1/pallas_call | solution.py:76
  216.1 1.5 collective-permute-start.6
  217.7 13.2 %features_2.1 = (bf16[2048,256]{1,0:T(8,128)(2,1)}, bf16[1024,2048]{1,0:T(8,128)(2,1)}, f32[256,1]{1,0:T(8,128)}) custom-call(f32[16,3,40,256]{3,2,1,0:T(8,128)} %copy-done.1, bf16[2048,640]{1,0:T(8,128)(2,1)} %subtract_convert_fusion.sel_ref, bf16[1024,2048]{1,0:T(8,128)(2,1)} %get-tuple-element.18.refs_0_), custom_call_target="tpu_custom_call", output_to_operand_aliasing={{1}: (2, {})} | custom-call | tf_op jit(solution)/shard_map/features_2/pallas_call | solution.py:76
  230.8 1.5 collective-permute-start.3
  232.3 59.2 %all-to-all-done.x_ref = f32[16,3,40,256]{3,2,1,0:T(8,128)S(1)} async-done(((f32[16,3,40,256]{3,2,1,0:T(8,128)}), f32[16,3,40,256]{3,2,1,0:T(8,128)S(1)}, u32[]{:S(2)}, u32[]{:S(2)}) %all-to-all-start) | async-done | bytes 1966112 | tf_op jit(solution)/shard_map/all_to_all | solution.py:162
  291.5 1.3 copy-done
  292.8 13.2 %features_3.1 = (bf16[2048,256]{1,0:T(8,128)(2,1)}, bf16[1024,2048]{1,0:T(8,128)(2,1)}, f32[256,1]{1,0:T(8,128)}) custom-call(f32[16,3,40,256]{3,2,1,0:T(8,128)} %copy-done, bf16[2048,640]{1,0:T(8,128)(2,1)} %subtract_convert_fusion.sel_ref, bf16[1024,2048]{1,0:T(8,128)(2,1)} %get-tuple-element.19.refs_0_), custom_call_target="tpu_custom_call", output_to_operand_aliasing={{1}: (2, {})} | custom-call | tf_op jit(solution)/shard_map/features_3/pallas_call | solution.py:76
  306.0 5.9 %collective-permute-start = (bf16[2048,256]{1,0:T(8,128)(2,1)}, bf16[2048,256]{1,0:T(8,128)(2,1)S(1)}, u32[]{:S(2)}, u32[]{:S(2)}) collective-permute-start(bf16[2048,256]{1,0:T(8,128)(2,1)} %get-tuple-element.25), channel_id=1, source_target_pairs={{0,4},{1,5},{2,6},{3,7},{4,8},{5,9},{6,10},{7,11},{8,12},{9,13},{1... | collective-permute-start | bytes 3145736 | tf_op jit(solution)/shard_map/ppermute | solution.py:17
  311.9 0.0 collective-permute-done.9.v4_ref
  311.9 1.7 select_bitcast_fusion
  313.7 3.3 collective-permute-start.10
  317.0 0.0 collective-permute-done.6.v4_ref
  317.0 1.4 select_bitcast_fusion.1
  318.3 0.2 collective-permute-start.7
  318.5 0.0 collective-permute-done.3.v4_ref
  318.5 1.5 select_bitcast_fusion.2
  320.0 1.9 collective-permute-start.4
  321.9 13.9 %collective-permute-done.v4_ref = bf16[2048,256]{1,0:T(8,128)(2,1)S(1)} collective-permute-done((bf16[2048,256]{1,0:T(8,128)(2,1)}, bf16[2048,256]{1,0:T(8,128)(2,1)S(1)}, u32[]{:S(2)}, u32[]{:S(2)}) %collective-permute-start) | collective-permute-done | bytes 1048608 | tf_op jit(solution)/shard_map/ppermute | solution.py:17
  335.8 0.1 select_bitcast_fusion.3
  335.9 0.8 copy-done.4
  336.8 2.6 collective-permute-start.1
  339.4 1.6 collective-permute-done.10.v2_ref
  341.0 1.7 pad_maximum_fusion.3
  342.6 0.0 collective-permute-start.11
  342.6 20.8 %collective-permute-done.7.v2_ref = bf16[2048,256]{1,0:T(8,128)(2,1)S(1)} collective-permute-done((bf16[2048,256]{1,0:T(8,128)(2,1)S(1)}, bf16[2048,256]{1,0:T(8,128)(2,1)S(1)}, u32[]{:S(2)}, u32[]{:S(2)}) %collective-permute-start.7) | collective-permute-done | bytes 1048608 | tf_op jit(solution)/shard_map/ppermute | solution.py:17
  363.4 1.6 pad_maximum_fusion.2
  365.0 0.0 copy-done.6
  365.1 0.0 collective-permute-start.8
  365.1 20.8 %collective-permute-done.4.v2_ref = bf16[2048,256]{1,0:T(8,128)(2,1)S(1)} collective-permute-done((bf16[2048,256]{1,0:T(8,128)(2,1)S(1)}, bf16[2048,256]{1,0:T(8,128)(2,1)S(1)}, u32[]{:S(2)}, u32[]{:S(2)}) %collective-permute-start.4) | collective-permute-done | bytes 1048608 | tf_op jit(solution)/shard_map/ppermute | solution.py:17
  385.9 0.2 pad_maximum_fusion.1
  386.1 0.8 copy-done.7
  386.9 0.0 collective-permute-start.5
  386.9 20.9 %collective-permute-done.1.v2_ref = bf16[2048,256]{1,0:T(8,128)(2,1)S(1)} collective-permute-done((bf16[2048,256]{1,0:T(8,128)(2,1)S(1)}, bf16[2048,256]{1,0:T(8,128)(2,1)S(1)}, u32[]{:S(2)}, u32[]{:S(2)}) %collective-permute-start.1) | collective-permute-done | bytes 1048608 | tf_op jit(solution)/shard_map/ppermute | solution.py:17
  407.8 1.5 pad_maximum_fusion
  409.3 0.2 copy-done.8
  409.5 1.0 copy.21
  410.5 0.1 copy.20
  410.6 0.1 copy.19
  410.6 0.1 copy.18
  410.7 1.1 copy.25.norm_ref
  411.8 0.0 collective-permute-done.11.vx_ref
  411.8 9.0 %distances_0.1.refs_0_ = bf16[4,1024,1024]{2,1,0:T(8,128)(2,1)} custom-call(s32[1]{0:T(128)} %bitcast.bit_ref, bf16[1024,2048]{1,0:T(8,128)(2,1)} %get-tuple-element.20.own_ref, f32[1024,1]{1,0:T(8,128)} %copy.25.norm_ref, bf16[2048,256]{1,0:T(8,128)(2,1)} %copy-done.3, bf16[2048,256]{1,0:T(8,128)(2,1)} %copy-done.5, ...), custom_call_target="tpu_custom_call" | custom-call | tf_op jit(solution)/shard_map/distances_0/pallas_call | solution.py:138
  420.8 0.0 collective-permute-done.8.vx_ref
  420.8 9.0 %distances_1.1.refs_0_ = bf16[4,1024,1024]{2,1,0:T(8,128)(2,1)} custom-call(s32[1]{0:T(128)} %bitcast.bit_ref, bf16[1024,2048]{1,0:T(8,128)(2,1)} %get-tuple-element.20.own_ref, f32[1024,1]{1,0:T(8,128)} %copy.25.norm_ref, bf16[2048,256]{1,0:T(8,128)(2,1)} %collective-permute-done.6.v4_ref, ...), custom_call_target="tpu_custom_call", output_to_operand_aliasing={{}: (6, {})} | custom-call | tf_op jit(solution)/shard_map/distances_1/pallas_call | solution.py:138
  429.9 9.0 %distances_2.1.refs_0_ = bf16[4,1024,1024]{2,1,0:T(8,128)(2,1)} custom-call(s32[1]{0:T(128)} %bitcast.bit_ref, bf16[1024,2048]{1,0:T(8,128)(2,1)} %get-tuple-element.20.own_ref, f32[1024,1]{1,0:T(8,128)} %copy.25.norm_ref, bf16[2048,256]{1,0:T(8,128)(2,1)} %collective-permute-done.3.v4_ref, ...), custom_call_target="tpu_custom_call", output_to_operand_aliasing={{}: (6, {})} | custom-call | tf_op jit(solution)/shard_map/distances_2/pallas_call | solution.py:138
  438.9 0.0 collective-permute-done.2.vx_ref
  438.9 9.0 %distances_3.1 = bf16[4,1024,1024]{2,1,0:T(8,128)(2,1)} custom-call(s32[1]{0:T(128)} %bitcast.bit_ref, bf16[1024,2048]{1,0:T(8,128)(2,1)} %get-tuple-element.20.own_ref, f32[1024,1]{1,0:T(8,128)} %copy.25.norm_ref, bf16[2048,256]{1,0:T(8,128)(2,1)} %copy-done.4, bf16[2048,256]{1,0:T(8,128)(2,1)} %copy-done.8, ...), custom_call_target="tpu_custom_call", output_to_operand_aliasing={{}: (6, {})} | custom-call | tf_op jit(solution)/shard_map/distances_3/pallas_call | solution.py:138
  (32 shorter events, 0.1 us)
Async XLA Ops:
  28.3 46.1 %all-to-all-start.3 = ((f32[16,3,40,256]{3,2,1,0:T(8,128)}), f32[16,3,40,256]{3,2,1,0:T(8,128)S(1)}, u32[]{:S(2)}, u32[]{:S(2)}) async-start(f32[16,3,40,256]{3,2,1,0:T(8,128)} %bitcast.40), calls=%async_computation.3 | async-start | bytes 3932160 | tf_op jit(solution)/shard_map/all_to_all | solution.py:162
  74.5 14.7 %copy-start.2 = (f32[16,3,40,256]{3,2,1,0:T(8,128)}, f32[16,3,40,256]{3,2,1,0:T(8,128)S(1)}, u32[]{:S(2)}) copy-start(f32[16,3,40,256]{3,2,1,0:T(8,128)S(1)} %all-to-all-done.3.x_ref) | copy-start | bytes 5898244
  74.5 49.5 %all-to-all-start.2 = ((f32[16,3,40,256]{3,2,1,0:T(8,128)}), f32[16,3,40,256]{3,2,1,0:T(8,128)}, u32[]{:S(2)}, u32[]{:S(2)}) async-start(f32[16,3,40,256]{3,2,1,0:T(8,128)} %bitcast.39), calls=%async_computation.2 | async-start | bytes 3932160 | tf_op jit(solution)/shard_map/all_to_all | solution.py:162
  124.0 49.4 %all-to-all-start.1 = ((f32[16,3,40,256]{3,2,1,0:T(8,128)}), f32[16,3,40,256]{3,2,1,0:T(8,128)S(1)}, u32[]{:S(2)}, u32[]{:S(2)}) async-start(f32[16,3,40,256]{3,2,1,0:T(8,128)} %bitcast.38), calls=%async_computation.1 | async-start | bytes 3932160 | tf_op jit(solution)/shard_map/all_to_all | solution.py:162
  138.7 46.7 %copy-start.15 = (s32[2,2048]{1,0:T(2,128)S(1)}, s32[2,2048]{1,0:T(2,128)}, u32[]{:S(2)}) copy-start(s32[2,2048]{1,0:T(2,128)} %param.4) | copy-start | bytes 49156
  138.7 46.8 %copy-start.16 = (s32[640]{0:T(1024)S(1)}, s32[640]{0:T(1024)}, u32[]{:S(2)}) copy-start(s32[640]{0:T(1024)} %param.5) | copy-start | bytes 7684
  173.3 1.4 copy-start.1
  174.7 116.8 %all-to-all-start = ((f32[16,3,40,256]{3,2,1,0:T(8,128)}), f32[16,3,40,256]{3,2,1,0:T(8,128)S(1)}, u32[]{:S(2)}, u32[]{:S(2)}) async-start(f32[16,3,40,256]{3,2,1,0:T(8,128)} %bitcast.37), calls=%async_computation | async-start | bytes 3932160 | tf_op jit(solution)/shard_map/all_to_all | solution.py:162
  200.8 111.1 %collective-permute-start.9 = (bf16[2048,256]{1,0:T(8,128)(2,1)}, bf16[2048,256]{1,0:T(8,128)(2,1)S(1)}, u32[]{:S(2)}, u32[]{:S(2)}) collective-permute-start(bf16[2048,256]{1,0:T(8,128)(2,1)} %get-tuple-element.28), channel_id=1, source_target_pairs={{0,4},{1,5},{2,6},{3,7},{4,8},{5,9},{6,10},{7,11},{8,12},{9,13},{1... | collective-permute-start | bytes 3145736 | tf_op jit(solution)/shard_map/ppermute | solution.py:17
  216.1 100.8 %collective-permute-start.6 = (bf16[2048,256]{1,0:T(8,128)(2,1)}, bf16[2048,256]{1,0:T(8,128)(2,1)}, u32[]{:S(2)}, u32[]{:S(2)}) collective-permute-start(bf16[2048,256]{1,0:T(8,128)(2,1)} %get-tuple-element.27), channel_id=1, source_target_pairs={{0,4},{1,5},{2,6},{3,7},{4,8},{5,9},{6,10},{7,11},{8,12},{9,13},{1... | collective-permute-start | bytes 3145736 | tf_op jit(solution)/shard_map/ppermute | solution.py:17
  230.8 87.7 %collective-permute-start.3 = (bf16[2048,256]{1,0:T(8,128)(2,1)}, bf16[2048,256]{1,0:T(8,128)(2,1)}, u32[]{:S(2)}, u32[]{:S(2)}) collective-permute-start(bf16[2048,256]{1,0:T(8,128)(2,1)} %get-tuple-element.26), channel_id=1, source_target_pairs={{0,4},{1,5},{2,6},{3,7},{4,8},{5,9},{6,10},{7,11},{8,12},{9,13},{1... | collective-permute-start | bytes 3145736 | tf_op jit(solution)/shard_map/ppermute | solution.py:17
  291.5 1.3 copy-start
  306.0 10.9 %copy-start.9 = (bf16[2048,256]{1,0:T(8,128)(2,1)S(1)}, bf16[2048,256]{1,0:T(8,128)(2,1)}, u32[]{:S(2)}) copy-start(bf16[2048,256]{1,0:T(8,128)(2,1)} %get-tuple-element.27) | copy-start | bytes 3145732
  306.0 29.7 %collective-permute-start = (bf16[2048,256]{1,0:T(8,128)(2,1)}, bf16[2048,256]{1,0:T(8,128)(2,1)S(1)}, u32[]{:S(2)}, u32[]{:S(2)}) collective-permute-start(bf16[2048,256]{1,0:T(8,128)(2,1)} %get-tuple-element.25), channel_id=1, source_target_pairs={{0,4},{1,5},{2,6},{3,7},{4,8},{5,9},{6,10},{7,11},{8,12},{9,13},{1... | collective-permute-start | bytes 3145736 | tf_op jit(solution)/shard_map/ppermute | solution.py:17
  311.9 1.8 copy-start.3
  313.7 4.8 %copy-start.10 = (bf16[2048,256]{1,0:T(8,128)(2,1)S(1)}, bf16[2048,256]{1,0:T(8,128)(2,1)}, u32[]{:S(2)}) copy-start(bf16[2048,256]{1,0:T(8,128)(2,1)} %get-tuple-element.26) | copy-start | bytes 3145732
  313.7 27.3 %collective-permute-start.10 = (bf16[2048,256]{1,0:T(8,128)(2,1)S(1)}, bf16[2048,256]{1,0:T(8,128)(2,1)S(1)}, u32[]{:S(2)}, u32[]{:S(2)}) collective-permute-start(bf16[2048,256]{1,0:T(8,128)(2,1)S(1)} %get-tuple-element.34), channel_id=1, source_target_pairs={{0,2},{1,3},{2,0},{3,1},{4,6},{5,7},{6,4},{7,5},{8,10},{9,11},{10,... | collective-permute-start | bytes 3145736 | tf_op jit(solution)/shard_map/ppermute | solution.py:17
  318.3 17.5 %copy-start.11 = (bf16[2048,256]{1,0:T(8,128)(2,1)S(1)}, bf16[2048,256]{1,0:T(8,128)(2,1)}, u32[]{:S(2)}) copy-start(bf16[2048,256]{1,0:T(8,128)(2,1)} %get-tuple-element.25) | copy-start | bytes 3145732
  318.3 45.1 %collective-permute-start.7 = (bf16[2048,256]{1,0:T(8,128)(2,1)S(1)}, bf16[2048,256]{1,0:T(8,128)(2,1)S(1)}, u32[]{:S(2)}, u32[]{:S(2)}) collective-permute-start(bf16[2048,256]{1,0:T(8,128)(2,1)S(1)} %get-tuple-element.36), channel_id=1, source_target_pairs={{0,2},{1,3},{2,0},{3,1},{4,6},{5,7},{6,4},{7,5},{8,10},{9,11},{10,... | collective-permute-start | bytes 3145736 | tf_op jit(solution)/shard_map/ppermute | solution.py:17
  320.0 65.9 %collective-permute-start.4 = (bf16[2048,256]{1,0:T(8,128)(2,1)S(1)}, bf16[2048,256]{1,0:T(8,128)(2,1)S(1)}, u32[]{:S(2)}, u32[]{:S(2)}) collective-permute-start(bf16[2048,256]{1,0:T(8,128)(2,1)S(1)} %get-tuple-element.38), channel_id=1, source_target_pairs={{0,2},{1,3},{2,0},{3,1},{4,6},{5,7},{6,4},{7,5},{8,10},{9,11},{10,... | collective-permute-start | bytes 3145736 | tf_op jit(solution)/shard_map/ppermute | solution.py:17
  335.8 1.0 copy-start.4
  336.8 71.0 %collective-permute-start.1 = (bf16[2048,256]{1,0:T(8,128)(2,1)S(1)}, bf16[2048,256]{1,0:T(8,128)(2,1)S(1)}, u32[]{:S(2)}, u32[]{:S(2)}) collective-permute-start(bf16[2048,256]{1,0:T(8,128)(2,1)S(1)} %get-tuple-element.40), channel_id=1, source_target_pairs={{0,2},{1,3},{2,0},{3,1},{4,6},{5,7},{6,4},{7,5},{8,10},{9,11},{10,... | collective-permute-start | bytes 3145736 | tf_op jit(solution)/shard_map/ppermute | solution.py:17
  341.0 1.7 copy-start.5
  342.6 69.2 %collective-permute-start.11 = (bf16[2,2048,256]{2,1,0:T(8,128)(2,1)}, bf16[2,2048,256]{2,1,0:T(8,128)(2,1)}, u32[]{:S(2)}, u32[]{:S(2)}) collective-permute-start(bf16[2,2048,256]{2,1,0:T(8,128)(2,1)} %pad_maximum_fusion.3), channel_id=1, source_target_pairs={{0,1},{1,0},{2,3},{3,2},{4,5},{5,4},{6,7},{7,6},{8,9},{9,8},{10,11... | collective-permute-start | bytes 6291464 | tf_op jit(solution)/shard_map/ppermute | solution.py:17
  363.4 1.6 copy-start.6
  365.1 55.8 %collective-permute-start.8 = (bf16[2,2048,256]{2,1,0:T(8,128)(2,1)}, bf16[2,2048,256]{2,1,0:T(8,128)(2,1)}, u32[]{:S(2)}, u32[]{:S(2)}) collective-permute-start(bf16[2,2048,256]{2,1,0:T(8,128)(2,1)} %pad_maximum_fusion.2), channel_id=1, source_target_pairs={{0,1},{1,0},{2,3},{3,2},{4,5},{5,4},{6,7},{7,6},{8,9},{9,8},{10,11... | collective-permute-start | bytes 6291464 | tf_op jit(solution)/shard_map/ppermute | solution.py:17
  385.9 1.0 copy-start.7
  386.9 43.0 %collective-permute-start.5 = (bf16[2,2048,256]{2,1,0:T(8,128)(2,1)S(1)}, bf16[2,2048,256]{2,1,0:T(8,128)(2,1)}, u32[]{:S(2)}, u32[]{:S(2)}) collective-permute-start(bf16[2,2048,256]{2,1,0:T(8,128)(2,1)S(1)} %pad_maximum_fusion.1), channel_id=1, source_target_pairs={{0,1},{1,0},{2,3},{3,2},{4,5},{5,4},{6,7},{7,6},{8,9},{9,8},{10,11... | collective-permute-start | bytes 6291464 | tf_op jit(solution)/shard_map/ppermute | solution.py:17
  407.8 1.7 copy-start.8
  407.8 2.7 copy-start.14
  407.8 2.7 copy-start.13
  407.8 2.8 copy-start.12
  409.5 29.4 %collective-permute-start.2 = (bf16[2,2048,256]{2,1,0:T(8,128)(2,1)}, bf16[2,2048,256]{2,1,0:T(8,128)(2,1)}, u32[]{:S(2)}, u32[]{:S(2)}) collective-permute-start(bf16[2,2048,256]{2,1,0:T(8,128)(2,1)} %pad_maximum_fusion), channel_id=1, source_target_pairs={{0,1},{1,0},{2,3},{3,2},{4,5},{5,4},{6,7},{7,6},{8,9},{9,8},{10,11... | collective-permute-start | bytes 6291464 | tf_op jit(solution)/shard_map/ppermute | solution.py:17
